TPU v7x, 32 devices: a whole 2x2x4 slice. The times are simulated.
32 devices in a mesh: groups: 2 (over y), ctx: 4 (over z), ch: 4 (over x, core).
Axes of the slice: x: 2, y: 2, z: 4, core: 2. Of those that a mesh axis runs over, the one named last changes fastest.
Arguments:
- projections: bfloat16 [1024, 3, 4096], P(('groups', 'ctx'), None, 'ch'), parts along dimension 0, may hold values from -6 to 6
- short_taps: float32 [3, 3, 4096], P(None, None, 'ch'), may hold values from -3 to 3
- residues: float32 [4096, 16], P(('ch', 'ctx')), may hold values from -2 to 2
- decay_rates: float32 [4096, 16], P(('ch', 'ctx')), may hold values from 0.25 to 16
- skip_gain: float32 [4096], P(('ch', 'ctx')), may hold values from -3 to 3
- grad_mixed: bfloat16 [1024, 2048], P(('groups', 'ctx'), 'ch'), parts along dimension 0, may hold values from -6 to 6
- out_weight: bfloat16 [4096, 2048], P('ch', 'ctx'), may hold values from -0.09375 to 0.09375
Outputs:
- grad_projections: bfloat16 [1024, 3, 4096], P(('groups', 'ctx'), None, 'ch'), parts along dimension 0
- grad_short: float32 [6, 3, 4096], P('groups', None, 'ch'), parts along dimension 0
- grad_skip: float32 [8192], P(('groups', 'ch', 'ctx')), parts along dimension 0
- grad_residues: float32 [8192, 16], P(('groups', 'ch', 'ctx')), parts along dimension 0
- grad_log_rates: float32 [8192, 16], P(('groups', 'ch', 'ctx')), parts along dimension 0
- grad_weight: float32 [8192, 2048], P(('groups', 'ch'), 'ctx'), parts along dimension 0
There are 2 independent parts, one for each index of `groups`. A program takes and returns all parts, laid end to end along the dimension named above; an argument that names none is the same for every part. Nothing has to cross between parts.
All inputs are finite; a program needn't handle non-finite values.
Results may differ from a plain program's by a relative error of at most 0.006.
Values may be sent and summed in bfloat16 or wider, within the bound.
A program may use at most 64 MiB of HBM per device.

v0:
```python
from functools import partial
import math
import jax
import jax.numpy as jnp
from jax import lax
from jax.sharding import PartitionSpec as P

SHORT = 3


def from_behind(x, axis, by):
    peers = lax.axis_size(axis)
    pairs = [(i, i + by) for i in range(peers) if 0 <= i + by < peers]
    return lax.ppermute(x, axis, pairs)


def make_filter(residues, decay_rates, seq_len):
    positions = jnp.arange(seq_len, dtype=jnp.float32) / seq_len
    amplitude = residues * jnp.sqrt(2.0 * decay_rates / seq_len)
    basis = jnp.exp(-decay_rates[:, :, None] * positions[None, None, :])
    return jnp.einsum("cn,cnt->ct", amplitude, basis, precision=lax.Precision.HIGHEST)


def circle(rows_count, cols_count, period):
    left_idx = jnp.arange(rows_count, dtype=jnp.int32)[:, None]
    right_idx = jnp.arange(cols_count, dtype=jnp.int32)[None, :]
    angle = (left_idx * right_idx % period).astype(jnp.float32) * (2.0 * math.pi / period)
    return (jnp.cos(angle), jnp.sin(angle))


def spectral_tables(length):
    factor_a = 1
    while factor_a * factor_a * 4 <= length and length % (factor_a * 2) == 0:
        factor_a = factor_a * 2
    factor_b = length // factor_a
    a_cos, a_sin = circle(factor_a, factor_a, factor_a)
    b_cos, b_sin = circle(factor_b, factor_b, factor_b)
    t_cos, t_sin = circle(factor_a, factor_b, length)
    return (length, factor_a, factor_b, a_cos, a_sin, b_cos, b_sin, t_cos, t_sin)


def forward_dft(signal, tables):
    length, factor_a, factor_b, a_cos, a_sin, b_cos, b_sin, t_cos, t_sin = tables
    highest = lax.Precision.HIGHEST
    channels, seq_len = signal.shape
    grid = jnp.pad(signal, ((0, 0), (0, length - seq_len))).reshape(channels, factor_a, factor_b)
    part_real = jnp.einsum("ka,cab->ckb", a_cos, grid, precision=highest)
    part_imag = -jnp.einsum("ka,cab->ckb", a_sin, grid, precision=highest)
    turn_real = part_real * t_cos + part_imag * t_sin
    turn_imag = part_imag * t_cos - part_real * t_sin
    out_real = jnp.einsum("ckb,bm->ckm", turn_real, b_cos, precision=highest) + jnp.einsum(
        "ckb,bm->ckm", turn_imag, b_sin, precision=highest
    )
    out_imag = jnp.einsum("ckb,bm->ckm", turn_imag, b_cos, precision=highest) - jnp.einsum(
        "ckb,bm->ckm", turn_real, b_sin, precision=highest
    )
    return (out_real, out_imag)


def inverse_dft(spec_real, spec_imag, seq_len, tables):
    length, factor_a, factor_b, a_cos, a_sin, b_cos, b_sin, t_cos, t_sin = tables
    highest = lax.Precision.HIGHEST
    channels = spec_real.shape[0]
    mid_real = jnp.einsum("ckm,mb->ckb", spec_real, b_cos, precision=highest) - jnp.einsum(
        "ckm,mb->ckb", spec_imag, b_sin, precision=highest
    )
    mid_imag = jnp.einsum("ckm,mb->ckb", spec_imag, b_cos, precision=highest) + jnp.einsum(
        "ckm,mb->ckb", spec_real, b_sin, precision=highest
    )
    turn_real = mid_real * t_cos - mid_imag * t_sin
    turn_imag = mid_imag * t_cos + mid_real * t_sin
    values = jnp.einsum("ak,ckb->cab", a_cos, turn_real, precision=highest) - jnp.einsum(
        "ak,ckb->cab", a_sin, turn_imag, precision=highest
    )
    return values.reshape(channels, length)[:, :seq_len] / length


def short_mix(extended, short_taps, tokens):
    running = jnp.zeros((tokens,) + extended.shape[1:], jnp.float32)
    for lag_index in range(SHORT):
        start_row = SHORT - 1 - lag_index
        running = running + short_taps[lag_index] * extended[start_row : start_row + tokens]
    return running


def mix_long(gate_cols, spec_h, gain, seq_len, tables):
    gate_f = gate_cols.astype(jnp.float32)
    u_real, u_imag = forward_dft(gate_f, tables)
    prod_real = spec_h[0] * u_real - spec_h[1] * u_imag
    prod_imag = spec_h[0] * u_imag + spec_h[1] * u_real
    mix_cols = (inverse_dft(prod_real, prod_imag, seq_len, tables) + gain[:, None] * gate_f).astype(
        jnp.bfloat16
    )
    return (mix_cols, (u_real, u_imag))


def grad_long(grad_cols_in, gate_cols, spec_u, spec_h, gain, seq_len, tables):
    grad_f = grad_cols_in.astype(jnp.float32)
    g_real, g_imag = forward_dft(grad_f, tables)
    back_real = spec_h[0] * g_real + spec_h[1] * g_imag
    back_imag = spec_h[0] * g_imag - spec_h[1] * g_real
    grad_cols = (
        inverse_dft(back_real, back_imag, seq_len, tables) + gain[:, None] * grad_f
    ).astype(jnp.bfloat16)
    corr_real = g_real * spec_u[0] + g_imag * spec_u[1]
    corr_imag = g_imag * spec_u[0] - g_real * spec_u[1]
    grad_filter = inverse_dft(corr_real, corr_imag, seq_len, tables)
    skip_sum = jnp.sum(grad_f * gate_cols.astype(jnp.float32), axis=1)
    return (grad_cols, grad_filter, skip_sum)


def body(projections, short_taps, residues, decay_rates, skip_gain, grad_mixed, out_weight):
    tokens = projections.shape[0]
    seq_len = tokens * lax.axis_size("ctx")
    norm_factor = math.sqrt(seq_len)
    tables = spectral_tables(2 * seq_len)
    earlier = from_behind(projections[tokens - SHORT + 1 :], "ctx", 1)
    ext_proj = jnp.concatenate([earlier, projections], axis=0)
    mixed_in = short_mix(ext_proj, short_taps, tokens)
    query_rows = mixed_in[:, 0]
    key_rows = mixed_in[:, 1]
    value_rows = mixed_in[:, 2]
    gated_rows = (key_rows * value_rows).astype(jnp.bfloat16)
    long_filter, filter_vjp = jax.vjp(partial(make_filter, seq_len=seq_len), residues, decay_rates)
    spec_h = forward_dft(long_filter, tables)
    out_rows = lax.all_gather(grad_mixed, "ch", axis=1, tiled=True)
    grad_out = lax.dot_general(
        out_rows,
        lax.all_gather(out_weight, "ctx", axis=1, tiled=True),
        (((1,), (1,)), ((), ())),
        preferred_element_type=jnp.float32,
    )
    grad_y = (grad_out * query_rows).astype(jnp.bfloat16)
    gate_cols, grad_cols_in = (
        lax.all_to_all(gated_rows.T, "ctx", split_axis=0, concat_axis=1, tiled=True),
        lax.all_to_all(grad_y.T, "ctx", split_axis=0, concat_axis=1, tiled=True),
    )
    mix_cols, spec_u = mix_long(gate_cols, spec_h, skip_gain, seq_len, tables)
    grad_cols, grad_filter, skip_sum = grad_long(
        grad_cols_in, gate_cols, spec_u, spec_h, skip_gain, seq_len, tables
    )
    returned = (
        lax.all_to_all(mix_cols, "ctx", split_axis=1, concat_axis=0, tiled=True),
        lax.all_to_all(grad_cols, "ctx", split_axis=1, concat_axis=0, tiled=True),
    )
    mix_rows = returned[0].T
    grad_gated = returned[1].T
    grad_res, grad_rate = filter_vjp(grad_filter)
    grad_residues = grad_res / norm_factor
    grad_log_rates = grad_rate * decay_rates / norm_factor
    grad_skip = skip_sum / norm_factor
    mixed_out = (query_rows * mix_rows).astype(jnp.bfloat16)
    grad_mix = jnp.stack(
        [grad_out * mix_rows, grad_gated * value_rows, grad_gated * key_rows], axis=1
    )
    later = from_behind(grad_mix[: SHORT - 1], "ctx", -1)
    ext_grad = jnp.concatenate([grad_mix, later], axis=0)
    running = jnp.zeros(grad_mix.shape, jnp.float32)
    short_terms = []
    for lag_index in range(SHORT):
        running = running + short_taps[lag_index] * ext_grad[lag_index : lag_index + tokens]
        start_row = SHORT - 1 - lag_index
        short_terms.append(jnp.sum(grad_mix * ext_proj[start_row : start_row + tokens], axis=0))
    grad_projections = running.astype(jnp.bfloat16)
    grad_short = lax.psum(jnp.stack(short_terms, axis=0), "ctx") / norm_factor
    partial_term = lax.dot_general(
        mixed_out, out_rows, (((0,), (0,)), ((), ())), preferred_element_type=jnp.float32
    )
    weight_sum = lax.psum_scatter(partial_term, "ctx", scatter_dimension=1, tiled=True)
    grad_weight = weight_sum / norm_factor
    return (grad_projections, grad_short, grad_skip, grad_residues, grad_log_rates, grad_weight)


def solution(mesh):
    return jax.shard_map(
        body,
        mesh=mesh,
        in_specs=(
            P(("groups", "ctx"), None, "ch"),
            P(None, None, "ch"),
            P(("ch", "ctx"), None),
            P(("ch", "ctx"), None),
            P(("ch", "ctx")),
            P(("groups", "ctx"), "ch"),
            P("ch", "ctx"),
        ),
        out_specs=(
            P(("groups", "ctx"), None, "ch"),
            P("groups", None, "ch"),
            P(("groups", "ch", "ctx")),
            P(("groups", "ch", "ctx"), None),
            P(("groups", "ch", "ctx"), None),
            P(("groups", "ch"), "ctx"),
        ),
        check_vma=False,
    )
```

profile of v0, /device:TPU:0, one launch (start us, length us, event | category | flops | bytes accessed | tf_op | source)
XLA Modules:
  0.0 378.1 jit_solution(4330585628768449797)
XLA Ops:
  8.7 4.9 %collective-permute-start = (bf16[2,3,1024]{2,0,1:T(2,128)(2,1)S(1)}, bf16[2,3,1024]{2,0,1:T(2,128)(2,1)S(1)}, u32[]{:S(2)}, u32[]{:S(2)}) collective-permute-start(bf16[2,3,1024]{2,0,1:T(2,128)(2,1)S(1)} %slice.52), channel_id=1, source_target_pairs={{0,4},{4,8},{8,12},{1,5},{5,9},{9,13},{2,6},{6,10},{10,14},{3,7},{... | collective-permute-start | bytes 36872 | tf_op jit(solution)/shard_map/ppermute | solution.py:14
  13.7 7.4 %all_gather.6 = bf16[128,2048]{1,0:T(8,128)(2,1)S(1)} all-gather(bf16[128,512]{1,0:T(8,128)(2,1)} %param.12), channel_id=1, replica_groups=mesh['groups'=2,'ctx'=4,'ch'=4] {'ch'}, dimensions={1}, use_global_device_ids=true | all-gather | bytes 655360 | tf_op jit(solution)/shard_map/all_gather | solution.py:126
  21.7 71.3 %all-gather.2.cloned.1.call-done = bf16[1024,2048]{1,0:T(8,128)(2,1)} async-done(((bf16[1024,512]{1,0:T(8,128)(2,1)}), bf16[1024,2048]{1,0:T(8,128)(2,1)}) %all-gather.2.cloned.1.call-update) | async-done | bytes 4194320 | tf_op jit(solution)/shard_map/all_gather | solution.py:129
  93.1 4.5 %multiply_convert_fusion.1 = (bf16[128,1024]{1,0:T(8,128)(2,1)S(1)}, bf16[128,1024]{1,0:T(8,128)(2,1)S(1)}, f32[128,1024]{1,0:T(8,128)}) fusion(f32[128,3,1024]{2,0,1:T(8,128)S(1)} %fusion.1, bf16[128,2048]{1,0:T(8,128)(2,1)S(1)} %all_gather.6, bf16[1024,2048]{1,0:T(8,128)(2,1)} %all-gather.2.cloned.1.call-done), kind=kOutput, calls=%fused_computation.133 | convolution fusion | flops 537395200 | bytes 7340032 | tf_op jit(solution)/shard_map/dot_general | solution.py:127
  98.4 3.4 all-to-all-start.2
  104.3 6.7 %all-to-all-done.2 = bf16[4,256,128]{1,2,0:T(8,128)(2,1)S(1)} async-done(((bf16[4,256,128]{1,2,0:T(8,128)(2,1)}), bf16[4,256,128]{1,2,0:T(8,128)(2,1)S(1)}, u32[]{:S(2)}, u32[]{:S(2)}) %all-to-all-start.2) | async-done | bytes 262176 | tf_op jit(solution)/shard_map/all_to_all | solution.py:136
  110.9 3.4 all-to-all-start
  115.1 2.7 fusion.10
  117.7 2.7 convolution_bitcast_fusion
  123.1 2.1 multiply_add_fusion.4
  137.8 3.1 multiply_add_fusion
  145.6 3.7 fusion.17
  149.3 3.7 fusion.8
  154.5 2.0 copy.328
  156.5 6.5 %multiply_reduce_fusion.2 = (f32[256,16]{1,0:T(8,128)}, f32[256,512]{1,0:T(8,128)}) fusion(f32[256,16]{1,0:T(8,128)} %copy.327, f32[256,512]{1,0:T(8,128)} %copy.328, f32[512]{0:T(512)S(1)} %iota_multiply_fusion.1, f32[256,16]{1,0:T(8,128)} %copy.203), kind=kLoop, calls=%fused_computation.2 | loop fusion | flops 14544896 | bytes 1099776 | tf_op jit(solution)/shard_map/transpose(jvp())/reduce_sum | solution.py:20
  163.1 2.1 copy.273
  168.0 2.0 multiply_add_fusion.5
  175.4 2.4 multiply_subtract_fusion.3
  186.9 3.7 fusion.31
  190.6 3.9 %fusion.11 = f32[256,32,32]{0,1,2:T(8,128)S(1)} fusion(f32[256,32,32]{0,2,1:T(8,128)S(1)} %fusion.31, f32[32,32]{0,1:T(8,128)S(1)} %copy.207, f32[32,32]{0,1:T(8,128)S(1)} %copy.205, f32[256,32,32]{0,2,1:T(8,128)S(1)} %fusion.98, f32[256,32,32]{0,2,1:T(8,128)S(1)} %fusion.122, f32[256,32,32]{0,2,1:T(8,128)S(1)} %fusion.96, f32[256,32,32]{0,2,1:T(8,128)S(1)} %fusion.120), kind=kOutput, calls=%fused_computation.32 | convolution fusion | flops 102250496 | bytes 6299648 | tf_op jit(solution)/shard_map/ak,ckb->cab/dot_general | solution.py:72
  195.1 3.7 fusion.24
  198.8 3.7 fusion.9
  204.3 11.1 %all_to_all.52 = bf16[256,4,128]{0,2,1:T(8,128)(2,1)S(1)} all-to-all(bf16[256,4,128]{0,2,1:T(8,128)(2,1)S(1)} %bitcast.240), channel_id=1, replica_groups=mesh['groups'=2,'ctx'=4,'ch'=4] {'ctx'}, dimensions={1} | all-to-all | bytes 524288 | tf_op jit(solution)/shard_map/all_to_all | solution.py:143
  215.5 4.5 %fusion.80 = f32[1024,2048]{1,0:T(8,128)} fusion(bf16[128,2048]{1,0:T(8,128)(2,1)S(1)} %all_gather.6, f32[1024,128]{0,1:T(8,128)S(1)} %bitcast.230, f32[128,3,1024]{2,0,1:T(8,128)S(1)} %fusion.1), kind=kOutput, calls=%fused_computation.146 | convolution fusion | flops 537133056 | bytes 9961472 | tf_op jit(solution)/shard_map/dot_general | solution.py:166
  220.1 3.6 all-to-all-start.3
  223.7 3.7 multiply_reduce_fusion
  228.3 8.6 %all-to-all-done.3 = bf16[256,4,128]{0,2,1:T(8,128)(2,1)S(1)} async-done(((bf16[256,4,128]{0,2,1:T(8,128)(2,1)}), bf16[256,4,128]{0,2,1:T(8,128)(2,1)S(1)}, u32[]{:S(2)}, u32[]{:S(2)}) %all-to-all-start.3) | async-done | bytes 262176 | tf_op jit(solution)/shard_map/all_to_all | solution.py:144
  240.2 7.0 %collective-permute-done.1 = f32[2,3,1024]{2,0,1:T(2,128)S(1)} collective-permute-done((f32[2,3,1024]{2,0,1:T(2,128)S(1)}, f32[2,3,1024]{2,0,1:T(2,128)S(1)}, u32[]{:S(2)}, u32[]{:S(2)}) %collective-permute-start.1) | collective-permute-done | bytes 24608 | tf_op jit(solution)/shard_map/ppermute | solution.py:14
  247.4 2.0 fusion.3
  249.4 19.5 %psum.7 = f32[3,3,1024]{2,1,0:T(4,128)S(1)} all-reduce(f32[3,3,1024]{2,1,0:T(4,128)S(1)} %pad_maximum_fusion.3), channel_id=1, replica_groups=mesh['groups'=2,'ctx'=4,'ch'=4] {'ctx'}, use_global_device_ids=true, to_apply=%region_3.4 | all-reduce | flops 9216 | bytes 73728 | tf_op jit(solution)/shard_map/psum | solution.py:165
  269.6 98.2 %reduce-scatter.2.cloned.1.call-done = f32[1024,512]{1,0:T(8,128)} async-done(((f32[1024,2048]{1,0:T(8,128)}), f32[1024,512]{1,0:T(8,128)}) %reduce-scatter.2.cloned.1.call-update) | async-done | bytes 2097168 | tf_op jit(solution)/shard_map/reduce_scatter | solution.py:169
  367.8 3.2 broadcast_multiply_fusion
  (103 shorter events, 51.9 us)
Async XLA Ops:
  7.2 14.0 %copy-start.9 = (bf16[128,3,1024]{2,0,1:T(8,128)(2,1)S(1)}, bf16[128,3,1024]{2,0,1:T(8,128)(2,1)}, u32[]{:S(2)}) copy-start(bf16[128,3,1024]{2,0,1:T(8,128)(2,1)} %param.7) | copy-start | bytes 2359300
  7.2 13.9 %copy-start.15 = (f32[3,3,1024]{2,1,0:T(4,128)S(1)}, f32[3,3,1024]{2,1,0:T(4,128)}, u32[]{:S(2)}) copy-start(f32[3,3,1024]{2,1,0:T(4,128)} %param.8) | copy-start | bytes 110596
  7.2 85.9 %all-gather.2.cloned.1.call-start = ((), (), s32[]{:S(2)}) async-start(), calls=%async_computation.5 | async-start | bytes 5242880 | tf_op jit(solution)/shard_map/all_gather | solution.py:129
  8.7 12.4 %collective-permute-start = (bf16[2,3,1024]{2,0,1:T(2,128)(2,1)S(1)}, bf16[2,3,1024]{2,0,1:T(2,128)(2,1)S(1)}, u32[]{:S(2)}, u32[]{:S(2)}) collective-permute-start(bf16[2,3,1024]{2,0,1:T(2,128)(2,1)S(1)} %slice.52), channel_id=1, source_target_pairs={{0,4},{4,8},{8,12},{1,5},{5,9},{9,13},{2,6},{6,10},{10,14},{3,7},{... | collective-permute-start | bytes 36872 | tf_op jit(solution)/shard_map/ppermute | solution.py:14
  21.7 80.3 %copy-start.13 = (f32[256,16]{0,1:T(8,128)S(1)}, f32[256,16]{0,1:T(8,128)}, u32[]{:S(2)}) copy-start(f32[256,16]{0,1:T(8,128)} %param.10) | copy-start | bytes 49156
  21.7 80.3 %copy-start.14 = (f32[256,16]{0,1:T(8,128)S(1)}, f32[256,16]{0,1:T(8,128)}, u32[]{:S(2)}) copy-start(f32[256,16]{0,1:T(8,128)} %param.9) | copy-start | bytes 49156
  98.4 12.6 %all-to-all-start.2 = ((bf16[4,256,128]{1,2,0:T(8,128)(2,1)}), bf16[4,256,128]{1,2,0:T(8,128)(2,1)S(1)}, u32[]{:S(2)}, u32[]{:S(2)}) async-start(bf16[4,256,128]{1,2,0:T(8,128)(2,1)} %bitcast.222), calls=%async_computation.2 | async-start | bytes 524288 | tf_op jit(solution)/shard_map/all_to_all | solution.py:136
  110.9 10.3 %all-to-all-start = ((bf16[4,256,128]{1,2,0:T(8,128)(2,1)}), bf16[4,256,128]{1,2,0:T(8,128)(2,1)S(1)}, u32[]{:S(2)}, u32[]{:S(2)}) async-start(bf16[4,256,128]{1,2,0:T(8,128)(2,1)} %bitcast.223), calls=%async_computation | async-start | bytes 524288 | tf_op jit(solution)/shard_map/all_to_all | solution.py:135
  114.4 253.5 %reduce-scatter.2.cloned.1.call-start = ((), (), s32[]{:S(2)}) async-start(), calls=%async_computation.6 | async-start | bytes 10485760 | tf_op jit(solution)/shard_map/reduce_scatter | solution.py:169
  121.2 1.9 copy-start.4
  121.3 1.8 copy-start.6
  121.3 1.8 copy-start.7
  136.0 1.8 copy-start
  137.8 3.1 copy-start.2
  173.5 1.9 copy-start.1
  173.5 1.9 copy-start.3
  173.5 1.9 copy-start.8
  202.5 1.0 copy-start.5
  202.5 0.9 copy-start.16
  220.1 3.6 copy-start.11
  220.1 16.8 %all-to-all-start.3 = ((bf16[256,4,128]{0,2,1:T(8,128)(2,1)}), bf16[256,4,128]{0,2,1:T(8,128)(2,1)S(1)}, u32[]{:S(2)}, u32[]{:S(2)}) async-start(bf16[256,4,128]{0,2,1:T(8,128)(2,1)} %bitcast.54), calls=%async_computation.3 | async-start | bytes 524288 | tf_op jit(solution)/shard_map/all_to_all | solution.py:144
  223.6 3.8 %copy-start.12 = (f32[256,16]{1,0:T(8,128)S(1)}, f32[256,16]{1,0:T(8,128)}, u32[]{:S(2)}) copy-start(f32[256,16]{1,0:T(8,128)} %get-tuple-element.15) | copy-start | bytes 49156
  238.4 8.9 %collective-permute-start.1 = (f32[2,3,1024]{2,0,1:T(2,128)S(1)}, f32[2,3,1024]{2,0,1:T(2,128)S(1)}, u32[]{:S(2)}, u32[]{:S(2)}) collective-permute-start(f32[2,3,1024]{2,0,1:T(2,128)S(1)} %slice.72), channel_id=1, source_target_pairs={{4,0},{8,4},{12,8},{5,1},{9,5},{13,9},{6,2},{10,6},{14,10},{7,3},{... | collective-permute-start | bytes 73736 | tf_op jit(solution)/shard_map/ppermute | solution.py:14
  240.2 7.2 %copy-start.10 = (bf16[128,3,1024]{2,0,1:T(8,128)(2,1)S(1)}, bf16[128,3,1024]{2,0,1:T(8,128)(2,1)}, u32[]{:S(2)}) copy-start(bf16[128,3,1024]{2,0,1:T(8,128)(2,1)} %param.7) | copy-start | bytes 2359300
Sparse Core Ops, SparseCore 0:
  9.6 83.4 all-gather.1
  220.2 147.5 reduce-scatter.1
where the time goes:
time: 382 us; the launch traced here: 378 us
  waiting for transfers between devices  193 us (51%)
  matrix products  81.3 us (21%)
  blocking collectives  38.1 us (10%)
  other arithmetic  21.5 us (6%)
  starting transfers between devices  17.2 us (5%)
  between operations  15 us (4%)
  local copies, waits for them, and re-layouts  11.7 us (3%)
    reduce_scatter x1, waiting for transfers between devices, body(): lax.psum_scatter(partial_term, 'ctx', scatter_dimension=1, tiled=True)  98.2 us
    all_gather x1, waiting for transfers between devices, body(): lax.all_gather(out_weight, 'ctx', axis=1, tiled=True)  71.3 us
    psum x1, blocking collectives, body(): grad_short = lax.psum(jnp.stack(short_terms, axis=0), 'ctx') / norm_factor  19.5 us
    dot_general x3, matrix products, inverse_dft(): jnp.einsum('ak,ckb->cab', a_sin, turn_imag, precision=highest)  11.3 us
    all_to_all x1, blocking collectives, body(): lax.all_to_all(mix_cols, 'ctx', split_axis=1, concat_axis=0, tiled=True)  11.1 us
    dot_general x3, matrix products, inverse_dft(): jnp.einsum('ak,ckb->cab', a_cos, turn_real, precision=highest)  11.1 us
    all_to_all x1, waiting for transfers between devices, body(): lax.all_to_all(grad_cols, 'ctx', split_axis=1, concat_axis=0, tiled=True)  8.58 us
  transfers between devices with their start and end apart: 7, of which 6 were waited for; matrix products, arithmetic and copies ran while one was open for 5% of the time, Pallas kernels for 0%

commit v1 on v0

--- a/solution.py
+++ b/solution.py
@@ -6,6 +6,24 @@
 from jax.sharding import PartitionSpec as P
 
 SHORT = 3
+
+
+def ring_gather(value, axis, dim):
+    ways, here, step = (lax.axis_size(axis), lax.axis_index(axis), value.shape[dim])
+    lengths = [n * ways if d == dim else n for d, n in enumerate(value.shape)]
+    full = lax.dynamic_update_slice_in_dim(
+        jnp.zeros(lengths, value.dtype), value, here * step, axis=dim
+    )
+    going_up = going_down = value
+    for far in range(1, ways // 2 + 1):
+        going_up = lax.ppermute(going_up, axis, [(d, (d + 1) % ways) for d in range(ways)])
+        full = lax.dynamic_update_slice_in_dim(full, going_up, (here - far) % ways * step, axis=dim)
+        if 2 * far < ways:
+            going_down = lax.ppermute(going_down, axis, [(d, (d - 1) % ways) for d in range(ways)])
+            full = lax.dynamic_update_slice_in_dim(
+                full, going_down, (here + far) % ways * step, axis=dim
+            )
+    return full
 
 
 def from_behind(x, axis, by):
@@ -126,7 +144,7 @@
     out_rows = lax.all_gather(grad_mixed, "ch", axis=1, tiled=True)
     grad_out = lax.dot_general(
         out_rows,
-        lax.all_gather(out_weight, "ctx", axis=1, tiled=True),
+        ring_gather(out_weight, "ctx", 1),
         (((1,), (1,)), ((), ())),
         preferred_element_type=jnp.float32,
     )

time: 382 us -> 370 us (0.969)
  waiting for transfers between devices: 193 us -> 164 us
  local copies, waits for them, and re-layouts: 11.7 us -> 24.2 us
    all_gather x1 -> x0, waiting for transfers between devices: 71.3 us -> none  [body(): lax.all_gather(out_weight, 'ctx', axis=1, tiled=True)]
    ppermute x0 -> x3, waiting for transfers between devices: none -> 40.4 us  [the longest x2 40.4 us: ring_gather(): lax.ppermute(going_up, axis, [(d, (d + 1) % ways) for d in range(ways)])]
    dynamic_update_slice x0 -> x4, local copies, waits for them, and re-layouts: none -> 8.06 us  [the longest x2 4.64 us: ring_gather(): lax.dynamic_update_slice_in_dim(full, going_up, (here - far) % ways * ste...]
    ppermute x2, waiting for transfers between devices: 7.01 us -> 13.2 us  [from_behind(): return lax.ppermute(x, axis, pairs)]
    ppermute x0 -> x3, starting transfers between devices: none -> 5.17 us  [the longest x2 3.08 us: ring_gather(): lax.ppermute(going_up, axis, [(d, (d + 1) % ways) for d in range(ways)])]
  transfers between devices with their start and end apart: 7 -> 9, of which waited for: 6 -> 8; matrix products, arithmetic and copies ran while one was open for 5% -> 8% of each run, Pallas kernels for 0% -> 0%
where the time goes in v1:
time: 370 us; the launch traced here: 365 us
  waiting for transfers between devices  164 us (44%)
  matrix products  81 us (22%)
  blocking collectives  40.4 us (11%)
  local copies, waits for them, and re-layouts  24.2 us (7%)
  other arithmetic  21.1 us (6%)
  starting transfers between devices  19.2 us (5%)
  between operations  15 us (4%)
    reduce_scatter x1, waiting for transfers between devices, body(): lax.psum_scatter(partial_term, 'ctx', scatter_dimension=1, tiled=True)  99.9 us
    ppermute x2, waiting for transfers between devices, ring_gather(): lax.ppermute(going_up, axis, [(d, (d + 1) % ways) for d in range(ways)])  40.4 us
    psum x1, blocking collectives, body(): grad_short = lax.psum(jnp.stack(short_terms, axis=0), 'ctx') / norm_factor  21.5 us
    ppermute x2, waiting for transfers between devices, from_behind(): return lax.ppermute(x, axis, pairs)  13.2 us
    all_to_all x1, blocking collectives, body(): lax.all_to_all(mix_cols, 'ctx', split_axis=1, concat_axis=0, tiled=True)  11.3 us
    dot_general x3, matrix products, inverse_dft(): jnp.einsum('ak,ckb->cab', a_sin, turn_imag, precision=highest)  11.3 us
    dot_general x3, matrix products, inverse_dft(): jnp.einsum('ak,ckb->cab', a_cos, turn_real, precision=highest)  11 us
    all_gather x1, blocking collectives, body(): out_rows = lax.all_gather(grad_mixed, 'ch', axis=1, tiled=True)  7.61 us
  transfers between devices with their start and end apart: 9, of which 8 were waited for; matrix products, arithmetic and copies ran while one was open for 8% of the time, Pallas kernels for 0%

profile of v1, /device:TPU:0, one launch (start us, length us, event | category | flops | bytes accessed | tf_op | source)
XLA Modules:
  0.0 365.3 jit_solution(12339320621070315360)
XLA Ops:
  7.2 3.1 collective-permute-start
  15.0 21.6 %collective-permute-done = bf16[1024,512]{1,0:T(8,128)(2,1)} collective-permute-done((bf16[1024,512]{1,0:T(8,128)(2,1)}, bf16[1024,512]{1,0:T(8,128)(2,1)}, u32[]{:S(2)}, u32[]{:S(2)}) %collective-permute-start) | collective-permute-done | bytes 1048608 | tf_op jit(solution)/shard_map/ppermute | solution.py:19
  36.6 7.6 %all_gather.3 = bf16[128,2048]{1,0:T(8,128)(2,1)S(1)} all-gather(bf16[128,512]{1,0:T(8,128)(2,1)} %param.12), channel_id=1, replica_groups=mesh['groups'=2,'ctx'=4,'ch'=4] {'ch'}, dimensions={1}, use_global_device_ids=true | all-gather | bytes 655360 | tf_op jit(solution)/shard_map/all_gather | solution.py:144
  44.2 2.5 broadcast_in_dim.2
  48.0 8.8 %collective-permute-done.3 = bf16[2,3,1024]{2,0,1:T(2,128)(2,1)S(1)} collective-permute-done((bf16[2,3,1024]{2,0,1:T(2,128)(2,1)S(1)}, bf16[2,3,1024]{2,0,1:T(2,128)(2,1)S(1)}, u32[]{:S(2)}, u32[]{:S(2)}) %collective-permute-start.3) | collective-permute-done | bytes 12320 | tf_op jit(solution)/shard_map/ppermute | solution.py:32
  57.3 2.3 constant_dynamic-update-slice_fusion.2
  59.7 2.3 constant_dynamic-update-slice_fusion.1
  62.0 18.7 %collective-permute-done.2 = bf16[1024,512]{1,0:T(8,128)(2,1)} collective-permute-done((bf16[1024,512]{1,0:T(8,128)(2,1)}, bf16[1024,512]{1,0:T(8,128)(2,1)}, u32[]{:S(2)}, u32[]{:S(2)}) %collective-permute-start.2) | collective-permute-done | bytes 1048608 | tf_op jit(solution)/shard_map/ppermute | solution.py:19
  83.1 4.6 %multiply_convert_fusion.1 = (bf16[128,1024]{1,0:T(8,128)(2,1)S(1)}, bf16[128,1024]{1,0:T(8,128)(2,1)S(1)}, f32[128,1024]{1,0:T(8,128)}) fusion(f32[128,3,1024]{2,0,1:T(8,128)S(1)} %fusion.1, bf16[1024,2048]{1,0:T(8,128)(2,1)} %constant_dynamic-update-slice_fusion, bf16[128,2048]{1,0:T(8,128)(2,1)S(1)} %all_gather.3), kind=kOutput, calls=%fused_computation.134 | convolution fusion | flops 537395200 | bytes 7340032 | tf_op jit(solution)/shard_map/dot_general | solution.py:145
  88.3 3.4 all-to-all-start.2
  94.2 4.2 %all-to-all-done.2 = bf16[4,256,128]{1,2,0:T(8,128)(2,1)S(1)} async-done(((bf16[4,256,128]{1,2,0:T(8,128)(2,1)}), bf16[4,256,128]{1,2,0:T(8,128)(2,1)S(1)}, u32[]{:S(2)}, u32[]{:S(2)}) %all-to-all-start.2) | async-done | bytes 262176 | tf_op jit(solution)/shard_map/all_to_all | solution.py:154
  98.5 3.4 all-to-all-start
  102.6 2.7 fusion.10
  105.3 2.7 convolution_bitcast_fusion
  125.2 3.1 multiply_add_fusion
  132.9 3.7 %fusion.17 = f32[256,32,32]{0,2,1:T(8,128)S(1)} fusion(f32[32,32]{0,1:T(8,128)S(1)} %copy.207, f32[32,32]{0,1:T(8,128)S(1)} %copy.205, f32[256,32,32]{0,2,1:T(8,128)S(1)} %fusion.88, f32[256,32,32]{0,2,1:T(8,128)S(1)} %fusion.112, f32[256,32,32]{0,2,1:T(8,128)S(1)} %fusion.86, f32[256,32,32]{0,2,1:T(8,128)S(1)} %fusion.110), kind=kOutput, calls=%fused_computation.54 | convolution fusion | flops 101988352 | bytes 5251072 | tf_op jit(solution)/shard_map/ak,ckb->cab/dot_general | solution.py:90
  136.6 3.7 %fusion.8 = f32[256,32,32]{0,1,2:T(8,128)S(1)} fusion(f32[256,32,32]{0,2,1:T(8,128)S(1)} %fusion.17, f32[32,32]{0,1:T(8,128)S(1)} %copy.207, f32[32,32]{0,1:T(8,128)S(1)} %copy.205, f32[256,32,32]{0,2,1:T(8,128)S(1)} %fusion.88, f32[256,32,32]{0,2,1:T(8,128)S(1)} %fusion.112, f32[256,32,32]{0,2,1:T(8,128)S(1)} %fusion.86, f32[256,32,32]{0,2,1:T(8,128)S(1)} %fusion.110), kind=kOutput, calls=%fused_computation.23 | convolution fusion | flops 102250496 | bytes 6299648 | tf_op jit(solution)/shard_map/ak,ckb->cab/dot_general | solution.py:90
  143.8 6.5 %multiply_reduce_fusion.2 = (f32[256,16]{1,0:T(8,128)}, f32[256,512]{1,0:T(8,128)}) fusion(f32[256,16]{1,0:T(8,128)} %copy.327, f32[256,512]{1,0:T(8,128)} %copy.328, f32[512]{0:T(512)S(1)} %iota_multiply_fusion.1, f32[256,16]{1,0:T(8,128)} %copy.203), kind=kLoop, calls=%fused_computation.2 | loop fusion | flops 14544896 | bytes 1099776 | tf_op jit(solution)/shard_map/transpose(jvp())/reduce_sum | solution.py:38
  162.6 2.4 multiply_subtract_fusion.3
  174.0 3.7 %fusion.31 = f32[256,32,32]{0,2,1:T(8,128)S(1)} fusion(f32[32,32]{0,1:T(8,128)S(1)} %copy.207, f32[32,32]{0,1:T(8,128)S(1)} %copy.205, f32[256,32,32]{0,2,1:T(8,128)S(1)} %fusion.98, f32[256,32,32]{0,2,1:T(8,128)S(1)} %fusion.122, f32[256,32,32]{0,2,1:T(8,128)S(1)} %fusion.96, f32[256,32,32]{0,2,1:T(8,128)S(1)} %fusion.120), kind=kOutput, calls=%fused_computation.74 | convolution fusion | flops 101988352 | bytes 5251072 | tf_op jit(solution)/shard_map/ak,ckb->cab/dot_general | solution.py:90
  177.7 3.9 %fusion.11 = f32[256,32,32]{0,1,2:T(8,128)S(1)} fusion(f32[256,32,32]{0,2,1:T(8,128)S(1)} %fusion.31, f32[32,32]{0,1:T(8,128)S(1)} %copy.207, f32[32,32]{0,1:T(8,128)S(1)} %copy.205, f32[256,32,32]{0,2,1:T(8,128)S(1)} %fusion.98, f32[256,32,32]{0,2,1:T(8,128)S(1)} %fusion.122, f32[256,32,32]{0,2,1:T(8,128)S(1)} %fusion.96, f32[256,32,32]{0,2,1:T(8,128)S(1)} %fusion.120), kind=kOutput, calls=%fused_computation.32 | convolution fusion | flops 102250496 | bytes 6299648 | tf_op jit(solution)/shard_map/ak,ckb->cab/dot_general | solution.py:90
  182.2 3.7 %fusion.24 = f32[256,32,32]{0,2,1:T(8,128)S(1)} fusion(f32[32,32]{0,1:T(8,128)S(1)} %copy.207, f32[32,32]{0,1:T(8,128)S(1)} %copy.205, f32[256,32,32]{0,2,1:T(8,128)S(1)} %fusion.92, f32[256,32,32]{0,2,1:T(8,128)S(1)} %fusion.116, f32[256,32,32]{0,2,1:T(8,128)S(1)} %fusion.90, f32[256,32,32]{0,2,1:T(8,128)S(1)} %fusion.114), kind=kOutput, calls=%fused_computation.63 | convolution fusion | flops 101988352 | bytes 5251072 | tf_op jit(solution)/shard_map/ak,ckb->cab/dot_general | solution.py:90
  185.9 3.7 %fusion.9 = f32[256,32,32]{0,1,2:T(8,128)S(1)} fusion(f32[256,32,32]{0,2,1:T(8,128)S(1)} %fusion.24, f32[32,32]{0,1:T(8,128)S(1)} %copy.207, f32[32,32]{0,1:T(8,128)S(1)} %copy.205, f32[256,32,32]{0,2,1:T(8,128)S(1)} %fusion.92, f32[256,32,32]{0,2,1:T(8,128)S(1)} %fusion.116, f32[256,32,32]{0,2,1:T(8,128)S(1)} %fusion.90, f32[256,32,32]{0,2,1:T(8,128)S(1)} %fusion.114), kind=kOutput, calls=%fused_computation.25 | convolution fusion | flops 102250496 | bytes 6299648 | tf_op jit(solution)/shard_map/ak,ckb->cab/dot_general | solution.py:90
  191.4 11.3 %all_to_all.52 = bf16[256,4,128]{0,2,1:T(8,128)(2,1)S(1)} all-to-all(bf16[256,4,128]{0,2,1:T(8,128)(2,1)S(1)} %bitcast.242), channel_id=1, replica_groups=mesh['groups'=2,'ctx'=4,'ch'=4] {'ctx'}, dimensions={1} | all-to-all | bytes 524288 | tf_op jit(solution)/shard_map/all_to_all | solution.py:161
  202.8 4.5 %fusion.80 = f32[1024,2048]{1,0:T(8,128)} fusion(bf16[128,2048]{1,0:T(8,128)(2,1)S(1)} %all_gather.3, f32[1024,128]{0,1:T(8,128)S(1)} %bitcast.232, f32[128,3,1024]{2,0,1:T(8,128)S(1)} %fusion.1), kind=kOutput, calls=%fused_computation.147 | convolution fusion | flops 537133056 | bytes 9961472 | tf_op jit(solution)/shard_map/dot_general | solution.py:184
  207.4 3.6 all-to-all-start.3
  210.9 4.2 %multiply_reduce_fusion = f32[256,16]{1,0:T(8,128)} fusion(f32[256,512]{1,0:T(8,128)S(1)} %copy-done.13, f32[512]{0:T(512)S(1)} %iota_multiply_fusion.1, f32[256,16]{1,0:T(8,128)} %copy.203), kind=kLoop, calls=%fused_computation | loop fusion | flops 6287360 | bytes 559104
  217.9 6.1 %all-to-all-done.3 = bf16[256,4,128]{0,2,1:T(8,128)(2,1)S(1)} async-done(((bf16[256,4,128]{0,2,1:T(8,128)(2,1)}), bf16[256,4,128]{0,2,1:T(8,128)(2,1)S(1)}, u32[]{:S(2)}, u32[]{:S(2)}) %all-to-all-start.3) | async-done | bytes 262176 | tf_op jit(solution)/shard_map/all_to_all | solution.py:162
  226.4 4.4 %collective-permute-done.4 = f32[2,3,1024]{2,0,1:T(2,128)S(1)} collective-permute-done((f32[2,3,1024]{2,0,1:T(2,128)S(1)}, f32[2,3,1024]{2,0,1:T(2,128)S(1)}, u32[]{:S(2)}, u32[]{:S(2)}) %collective-permute-start.4) | collective-permute-done | bytes 24608 | tf_op jit(solution)/shard_map/ppermute | solution.py:32
  233.0 21.5 %psum.7 = f32[3,3,1024]{2,1,0:T(4,128)S(1)} all-reduce(f32[3,3,1024]{2,1,0:T(4,128)S(1)} %pad_maximum_fusion.3), channel_id=1, replica_groups=mesh['groups'=2,'ctx'=4,'ch'=4] {'ctx'}, use_global_device_ids=true, to_apply=%region_3.4 | all-reduce | flops 9216 | bytes 73728 | tf_op jit(solution)/shard_map/psum | solution.py:183
  255.2 99.9 %reduce-scatter.2.cloned.1.call-done = f32[1024,512]{1,0:T(8,128)} async-done(((f32[1024,2048]{1,0:T(8,128)}), f32[1024,512]{1,0:T(8,128)}) %reduce-scatter.2.cloned.1.call-update) | async-done | bytes 2097168 | tf_op jit(solution)/shard_map/reduce_scatter | solution.py:187
  355.1 3.2 broadcast_multiply_fusion
  (113 shorter events, 69.4 us)
Async XLA Ops:
  7.2 29.5 %collective-permute-start = (bf16[1024,512]{1,0:T(8,128)(2,1)}, bf16[1024,512]{1,0:T(8,128)(2,1)}, u32[]{:S(2)}, u32[]{:S(2)}) collective-permute-start(bf16[1024,512]{1,0:T(8,128)(2,1)} %param.13), channel_id=1, source_target_pairs={{0,4},{4,8},{8,12},{12,0},{1,5},{5,9},{9,13},{13,1},{2,6},{6,10},{... | collective-permute-start | bytes 3145736 | tf_op jit(solution)/shard_map/ppermute | solution.py:19
  10.2 49.4 %collective-permute-start.1 = (bf16[1024,512]{1,0:T(8,128)(2,1)}, bf16[1024,512]{1,0:T(8,128)(2,1)}, u32[]{:S(2)}, u32[]{:S(2)}) collective-permute-start(bf16[1024,512]{1,0:T(8,128)(2,1)} %param.13), channel_id=1, source_target_pairs={{0,12},{4,0},{8,4},{12,8},{1,13},{5,1},{9,5},{13,9},{2,14},{6,2},{... | collective-permute-start | bytes 3145736 | tf_op jit(solution)/shard_map/ppermute | solution.py:22
  13.2 43.6 %collective-permute-start.3 = (bf16[2,3,1024]{2,0,1:T(2,128)(2,1)S(1)}, bf16[2,3,1024]{2,0,1:T(2,128)(2,1)S(1)}, u32[]{:S(2)}, u32[]{:S(2)}) collective-permute-start(bf16[2,3,1024]{2,0,1:T(2,128)(2,1)S(1)} %slice.52), channel_id=1, source_target_pairs={{0,4},{4,8},{8,12},{1,5},{5,9},{9,13},{2,6},{6,10},{10,14},{3,7},{... | collective-permute-start | bytes 36872 | tf_op jit(solution)/shard_map/ppermute | solution.py:32
  36.6 44.1 %collective-permute-start.2 = (bf16[1024,512]{1,0:T(8,128)(2,1)}, bf16[1024,512]{1,0:T(8,128)(2,1)}, u32[]{:S(2)}, u32[]{:S(2)}) collective-permute-start(bf16[1024,512]{1,0:T(8,128)(2,1)} %collective-permute-done), channel_id=1, source_target_pairs={{0,4},{4,8},{8,12},{12,0},{1,5},{5,9},{9,13},{13,1},{2,6},{6,10},{... | collective-permute-start | bytes 3145736 | tf_op jit(solution)/shard_map/ppermute | solution.py:19
  44.2 2.5 copy-start.12
  46.7 1.1 copy-start.16
  46.7 10.1 %copy-start.9 = (bf16[128,3,1024]{2,0,1:T(8,128)(2,1)S(1)}, bf16[128,3,1024]{2,0,1:T(8,128)(2,1)}, u32[]{:S(2)}) copy-start(bf16[128,3,1024]{2,0,1:T(8,128)(2,1)} %param.7) | copy-start | bytes 2359300
  83.0 8.9 %copy-start.14 = (f32[256,16]{0,1:T(8,128)S(1)}, f32[256,16]{0,1:T(8,128)}, u32[]{:S(2)}) copy-start(f32[256,16]{0,1:T(8,128)} %param.10) | copy-start | bytes 49156
  83.0 8.9 %copy-start.15 = (f32[256,16]{0,1:T(8,128)S(1)}, f32[256,16]{0,1:T(8,128)}, u32[]{:S(2)}) copy-start(f32[256,16]{0,1:T(8,128)} %param.9) | copy-start | bytes 49156
  88.3 10.2 %all-to-all-start.2 = ((bf16[4,256,128]{1,2,0:T(8,128)(2,1)}), bf16[4,256,128]{1,2,0:T(8,128)(2,1)S(1)}, u32[]{:S(2)}, u32[]{:S(2)}) async-start(bf16[4,256,128]{1,2,0:T(8,128)(2,1)} %bitcast.224), calls=%async_computation.2 | async-start | bytes 524288 | tf_op jit(solution)/shard_map/all_to_all | solution.py:154
  98.5 10.2 %all-to-all-start = ((bf16[4,256,128]{1,2,0:T(8,128)(2,1)}), bf16[4,256,128]{1,2,0:T(8,128)(2,1)S(1)}, u32[]{:S(2)}, u32[]{:S(2)}) async-start(bf16[4,256,128]{1,2,0:T(8,128)(2,1)} %bitcast.225), calls=%async_computation | async-start | bytes 524288 | tf_op jit(solution)/shard_map/all_to_all | solution.py:153
  101.9 253.2 %reduce-scatter.2.cloned.1.call-start = ((), (), s32[]{:S(2)}) async-start(), calls=%async_computation.5 | async-start | bytes 10485760 | tf_op jit(solution)/shard_map/reduce_scatter | solution.py:187
  108.7 1.9 copy-start.4
  108.7 1.8 copy-start.6
  108.8 1.8 copy-start.7
  123.4 1.8 copy-start
  125.1 3.1 copy-start.2
  160.7 1.8 copy-start.1
  160.7 1.8 copy-start.3
  160.7 1.8 copy-start.8
  189.6 1.0 copy-start.5
  189.6 0.9 copy-start.17
  207.3 3.6 copy-start.13
  207.4 16.6 %all-to-all-start.3 = ((bf16[256,4,128]{0,2,1:T(8,128)(2,1)}), bf16[256,4,128]{0,2,1:T(8,128)(2,1)S(1)}, u32[]{:S(2)}, u32[]{:S(2)}) async-start(bf16[256,4,128]{0,2,1:T(8,128)(2,1)} %bitcast.55), calls=%async_computation.3 | async-start | bytes 524288 | tf_op jit(solution)/shard_map/all_to_all | solution.py:162
  215.2 8.9 %copy-start.11 = (f32[128,1024]{1,0:T(8,128)S(1)}, f32[128,1024]{1,0:T(8,128)}, u32[]{:S(2)}) copy-start(f32[128,1024]{1,0:T(8,128)} %get-tuple-element.47) | copy-start | bytes 1572868
  224.6 6.2 %collective-permute-start.4 = (f32[2,3,1024]{2,0,1:T(2,128)S(1)}, f32[2,3,1024]{2,0,1:T(2,128)S(1)}, u32[]{:S(2)}, u32[]{:S(2)}) collective-permute-start(f32[2,3,1024]{2,0,1:T(2,128)S(1)} %slice.72), channel_id=1, source_target_pairs={{4,0},{8,4},{12,8},{5,1},{9,5},{13,9},{6,2},{10,6},{14,10},{7,3},{... | collective-permute-start | bytes 73736 | tf_op jit(solution)/shard_map/ppermute | solution.py:32
  226.4 4.6 %copy-start.10 = (bf16[128,3,1024]{2,0,1:T(8,128)(2,1)S(1)}, bf16[128,3,1024]{2,0,1:T(8,128)(2,1)}, u32[]{:S(2)}) copy-start(bf16[128,3,1024]{2,0,1:T(8,128)(2,1)} %param.7) | copy-start | bytes 2359300
Sparse Core Ops, SparseCore 0:
  207.5 147.5 reduce-scatter.1
